TPU v7x, 32 devices: a whole 2x2x4 slice. The times are simulated.
32 devices in a mesh: col: 8 (over z, core), row: 4 (over y, x).
Axes of the slice: x: 2, y: 2, z: 4, core: 2. Of those that a mesh axis runs over, the one named last changes fastest.
Arguments:
- matrix: float32 [4096, 4096], P('row', 'col'), may hold values from -64 to 64, as said below
- plan: int32 [3, 8], replicated, may hold values from 0 to 1
Outputs:
- rotated: float32 [4096, 4096], P('row', 'col')
- coupling: float32 [3], replicated
Inputs may be any that keep to these rules, and one draw needn't show every extreme that they name: Entries of the matrix are real numbers; column scales differ between columns.
All inputs are finite; a program needn't handle non-finite values.
Results may differ from a plain program's by a relative error of at most 0.0003.
Values sent between devices are 32-bit elements; how exact they have to be, the bound alone decides.
A program may use at most 128 MiB of HBM per device.

v0:
```python
import jax
import jax.numpy as jnp
from jax import lax
from jax.sharding import PartitionSpec as P

SWEEPS = 2
STEPS = 3
highest = lax.Precision.HIGHEST
eps = 1e-06


def from_behind(x, axis, by):
    count = lax.axis_size(axis)
    return lax.ppermute(x, axis, [(i, (i + by) % count) for i in range(count)])


def product(first, second):
    return jnp.dot(first, second, precision=highest, preferred_element_type=jnp.float32)


def sweep_rotation(gram):
    width = gram.shape[0]
    eye = jnp.eye(width, dtype=jnp.float32)
    upper = jnp.triu(jnp.ones((width, width), jnp.float32), 1)
    rotation = eye
    for sweep in range(SWEEPS):
        diag = jnp.diagonal(gram)
        ratio = gram / (diag[:, None] + diag[None, :] + eps) * upper
        skew_raw = ratio - ratio.T
        scale = jnp.maximum(jnp.sqrt(jnp.sum(skew_raw * skew_raw)), 1.0)
        skew = skew_raw / scale
        square = product(skew, skew)
        system = eye - square
        inverse = 4.0 / 3.0 * eye - 4.0 / 9.0 * system
        for turn in range(2):
            inverse = product(inverse, 2.0 * eye - product(system, inverse))
        qmat = product(eye - 2.0 * skew + square, inverse)
        gram = product(qmat.T, product(gram, qmat))
        if sweep == 0:
            rotation = qmat
        else:
            rotation = product(rotation, qmat)
    return (rotation, gram)


def local_product(first, second):
    return lax.dot_general(
        first,
        second,
        (((0,), (0,)), ((), ())),
        precision=highest,
        preferred_element_type=jnp.float32,
    )


def pass_on(send):
    return from_behind(send, "col", 1)


def rotate_local(pair, gram, block):
    rotation, turned = sweep_rotation(gram)
    moved = product(pair, rotation)
    cross_sq = jnp.sum(turned[:block, block:] * turned[:block, block:])
    diag_sq = jnp.sum(jnp.diagonal(turned) ** 2)
    return (moved, turned, cross_sq, diag_sq)


def tally_step(cross_sq, diag_sq):
    return lax.psum((cross_sq, diag_sq), "col")


def finish_tally(tallies):
    crosses = jnp.stack([entry[0] for entry in tallies])
    diagonals = jnp.stack([entry[1] for entry in tallies])
    return jnp.log(crosses / diagonals)


def on_device(matrix, plan):
    block = matrix.shape[1] // 2
    position = lax.axis_index("col")
    pair_count = plan.shape[1]
    picker = jnp.arange(pair_count, dtype=jnp.int32) == position
    pair = matrix
    tallies = []
    gram = lax.psum(local_product(pair, pair), "row")
    for step in range(STEPS):
        moved, turned, cross_sq, diag_sq = rotate_local(pair, gram, block)
        tallies.append(tally_step(cross_sq, diag_sq))
        flag = jnp.sum(jnp.where(picker, plan[step], 0)) == 1
        left = moved[:, :block]
        right = moved[:, block:]
        send = jnp.where(flag, right, left)
        keep = jnp.where(flag, left, right)
        if step + 1 < STEPS:
            send_gram = jnp.where(flag, turned[block:, block:], turned[:block, :block])
            keep_gram = jnp.where(flag, turned[:block, :block], turned[block:, block:])
            received, received_gram = from_behind((send, send_gram), "col", 1)
            pair = jnp.concatenate([keep, received], axis=1)
            cross = lax.psum(local_product(keep, received), "row")
            top_rows = jnp.concatenate([keep_gram, cross], axis=1)
            low_rows = jnp.concatenate([cross.T, received_gram], axis=1)
            gram = jnp.concatenate([top_rows, low_rows], axis=0)
        else:
            received = pass_on(send)
            pair = jnp.concatenate([keep, received], axis=1)
    return (pair, finish_tally(tallies))


def solution(mesh):
    in_specs = (P("row", "col"), P())
    out_specs = (P("row", "col"), P())
    return jax.shard_map(
        on_device, mesh=mesh, in_specs=in_specs, out_specs=out_specs, check_vma=False
    )
```

profile of v0, /device:TPU:0, one launch (start us, length us, event | category | flops | bytes accessed | tf_op | source)
XLA Modules:
  0.0 446.2 jit_solution(14428658945225685061)
XLA Ops:
  8.8 4.5 %fusion.148 = f32[512,512]{1,0:T(8,128)} fusion(f32[1024,512]{1,0:T(8,128)S(1)} %copy-done), kind=kOutput, calls=%fused_computation.235 | convolution fusion | flops 3221225472 | bytes 3145728 | tf_op jit(solution)/shard_map/dot_general | solution.py:47
  19.0 49.7 %all-reduce.5.cloned.1.call-done = f32[512,512]{1,0:T(8,128)} async-done(((f32[512,512]{1,0:T(8,128)}), f32[512,512]{1,0:T(8,128)}) %all-reduce.5.cloned.1.call-update) | async-done | bytes 1048592 | tf_op jit(solution)/shard_map/psum | solution.py:85
  68.7 9.3 %gather_fusion = f32[512]{0:T(512)S(1)} fusion(f32[512,512]{1,0:T(8,128)} %all-reduce.5.cloned.1.call-done, s32[512]{0:T(512)S(1)} %bitcast.137), kind=kCustom, calls=%fused_computation | custom fusion | bytes 8192 | tf_op jit(solution)/shard_map/jit(diagonal)/cond/branch_0_fun/gather | solution.py:27
  90.2 4.2 fusion.141
  108.2 4.5 %gather_fusion.1 = f32[512]{0:T(512)S(1)} fusion(f32[512,512]{1,0:T(8,128)S(1)} %fusion.151, s32[512]{0:T(512)S(1)} %bitcast.138), kind=kCustom, calls=%fused_computation.1 | custom fusion | bytes 8192 | tf_op jit(solution)/shard_map/jit(diagonal)/cond/branch_0_fun/gather | solution.py:27
  118.3 5.2 %fusion.87 = f32[512,512]{1,0:T(8,128)S(1)} fusion(f32[512,512]{0,1:T(8,128)} %get-tuple-element.18, f32[]{:T(128)S(6)} %max.19), kind=kOutput, calls=%fused_computation.160 | convolution fusion | flops 1610874880 | bytes 2097156 | tf_op jit(solution)/shard_map/dot_general | solution.py:18
  130.0 3.6 fusion.35
  141.7 6.7 %convolution_bitcast_fusion = f32[1024,512]{0,1:T(8,128)S(1)} fusion(f32[512,512]{1,0:T(8,128)S(1)} %fusion.153, f32[1024,512]{1,0:T(8,128)S(1)} %copy-done), kind=kOutput, calls=%fused_computation.50 | convolution fusion | flops 3221225472 | bytes 5242880 | tf_op jit(solution)/shard_map/dot_general | solution.py:18
  152.6 12.2 %collective-permute-done = f32[1024,256]{0,1:T(8,128)S(1)} collective-permute-done((f32[1024,256]{0,1:T(8,128)S(1)}, f32[1024,256]{0,1:T(8,128)S(1)}, u32[]{:S(2)}, u32[]{:S(2)}) %collective-permute-start) | collective-permute-done | bytes 1048608 | tf_op jit(solution)/shard_map/ppermute | solution.py:14
  168.8 40.1 %all-reduce.7.cloned.1.call-done = f32[256,256]{0,1:T(8,128)} async-done(((f32[256,256]{0,1:T(8,128)}), f32[256,256]{0,1:T(8,128)}) %all-reduce.7.cloned.1.call-update) | async-done | bytes 262160 | tf_op jit(solution)/shard_map/psum | solution.py:99
  211.3 4.7 %gather_fusion.2 = f32[512]{0:T(512)S(1)} fusion(f32[512,512]{0,1:T(8,128)S(1)} %maximum_maximum_fusion, s32[512]{0:T(512)S(1)} %bitcast.139), kind=kCustom, calls=%fused_computation.2 | custom fusion | bytes 8192 | tf_op jit(solution)/shard_map/jit(diagonal)/cond/branch_0_fun/gather | solution.py:27
  239.5 4.5 %gather_fusion.3 = f32[512]{0:T(512)S(1)} fusion(f32[512,512]{1,0:T(8,128)S(1)} %fusion.158, s32[512]{0:T(512)S(1)} %bitcast.140), kind=kCustom, calls=%fused_computation.3 | custom fusion | bytes 8192 | tf_op jit(solution)/shard_map/jit(diagonal)/cond/branch_0_fun/gather | solution.py:27
  249.6 5.1 %fusion.88 = f32[512,512]{1,0:T(8,128)S(1)} fusion(f32[512,512]{0,1:T(8,128)} %get-tuple-element.16, f32[]{:T(128)S(6)} %max.21), kind=kOutput, calls=%fused_computation.161 | convolution fusion | flops 1610874880 | bytes 2097156 | tf_op jit(solution)/shard_map/dot_general | solution.py:18
  261.2 3.6 fusion.25
  280.4 12.2 %collective-permute-done.2 = f32[1024,256]{0,1:T(8,128)S(1)} collective-permute-done((f32[1024,256]{0,1:T(8,128)S(1)}, f32[1024,256]{0,1:T(8,128)S(1)}, u32[]{:S(2)}, u32[]{:S(2)}) %collective-permute-start.2) | collective-permute-done | bytes 1048608 | tf_op jit(solution)/shard_map/ppermute | solution.py:14
  297.5 4.5 %gather_fusion.6 = f32[512]{0:T(512)S(1)} fusion(f32[512,512]{0,1:T(8,128)S(1)} %copy-done.6, s32[512]{0:T(512)S(1)} %bitcast.141), kind=kCustom, calls=%fused_computation.6 | custom fusion | bytes 8192 | tf_op jit(solution)/shard_map/jit(diagonal)/cond/branch_0_fun/gather | solution.py:64
  302.7 4.5 %gather_fusion.7 = f32[512]{0:T(512)S(1)} fusion(f32[512,512]{0,1:T(8,128)S(1)} %fusion.162, s32[512]{0:T(512)S(1)} %bitcast.142), kind=kCustom, calls=%fused_computation.7 | custom fusion | bytes 8192 | tf_op jit(solution)/shard_map/jit(diagonal)/cond/branch_0_fun/gather | solution.py:64
  307.3 29.5 %all-reduce.9.cloned.1.call-done = f32[256,256]{0,1:T(8,128)} async-done(((f32[256,256]{0,1:T(8,128)}), f32[256,256]{0,1:T(8,128)}) %all-reduce.9.cloned.1.call-update) | async-done | bytes 262160 | tf_op jit(solution)/shard_map/psum | solution.py:99
  339.8 5.0 %gather_fusion.4 = f32[512]{0:T(512)S(1)} fusion(f32[512,512]{0,1:T(8,128)S(1)} %maximum_maximum_fusion.1, s32[512]{0:T(512)S(1)} %bitcast.143), kind=kCustom, calls=%fused_computation.4 | custom fusion | bytes 8192 | tf_op jit(solution)/shard_map/jit(diagonal)/cond/branch_0_fun/gather | solution.py:27
  362.9 4.5 %gather_fusion.5 = f32[512]{0:T(512)S(1)} fusion(f32[512,512]{1,0:T(8,128)S(1)} %fusion.165, s32[512]{0:T(512)S(1)} %bitcast.144), kind=kCustom, calls=%fused_computation.5 | custom fusion | bytes 8192 | tf_op jit(solution)/shard_map/jit(diagonal)/cond/branch_0_fun/gather | solution.py:27
  379.8 4.5 %fusion.89 = f32[512,512]{1,0:T(8,128)S(1)} fusion(f32[]{:T(128)S(6)} %max.23, f32[512,512]{1,0:T(8,128)} %copy.58, f32[512,512]{1,0:T(8,128)} %copy.57), kind=kOutput, calls=%fused_computation.162 | convolution fusion | flops 1611923456 | bytes 3145732 | tf_op jit(solution)/shard_map/dot_general | solution.py:18
  405.4 4.5 %gather_fusion.8 = f32[512]{0:T(512)S(1)} fusion(f32[512,512]{1,0:T(8,128)S(1)} %fusion.169, s32[512]{0:T(512)S(1)} %bitcast.145), kind=kCustom, calls=%fused_computation.8 | custom fusion | bytes 8192 | tf_op jit(solution)/shard_map/jit(diagonal)/cond/branch_0_fun/gather | solution.py:64
  411.3 17.8 %all-reduce = (f32[1]{0:T(128)}, f32[1]{0:T(128)}, f32[1]{0:T(128)}, f32[1]{0:T(128)}, f32[1]{0:T(128)}, /*index=5*/f32[1]{0:T(128)}) all-reduce(f32[1]{0:T(128)} %bitcast.18, f32[1]{0:T(128)} %bitcast.17, f32[1]{0:T(128)} %bitcast.16, f32[1]{0:T(128)} %bitcast.15, f32[1]{0:T(128)} %bitcast.14, ...), channel_id=1, replica_groups=mesh['col'=8,'row'=4] {'col'}, use_global_device_ids=true, to_apply=%region_23.24 | all-reduce | flops 6 | bytes 48 | tf_op jit(solution)/shard_map/psum | solution.py:69
  429.1 4.3 fusion.96
  (209 shorter events, 175.7 us)
Async XLA Ops:
  7.2 61.5 %all-reduce.5.cloned.1.call-start = ((), (), s32[]{:S(2)}) async-start(), calls=%async_computation | async-start | bytes 2097152 | tf_op jit(solution)/shard_map/psum | solution.py:85
  13.3 195.6 %all-reduce.7.cloned.1.call-start = ((), (), s32[]{:S(2)}) async-start(), calls=%async_computation.1 | async-start | bytes 524288 | tf_op jit(solution)/shard_map/psum | solution.py:99
  78.0 3.7 copy-start.2
  130.0 3.6 copy-start.12
  148.7 16.1 %copy-start.9 = (f32[1024,256]{0,1:T(8,128)}, f32[1024,256]{0,1:T(8,128)S(1)}, u32[]{:S(2)}) copy-start(f32[1024,256]{0,1:T(8,128)S(1)} %get-tuple-element.24) | copy-start | bytes 3145732
  148.7 16.1 %collective-permute-start = (f32[1024,256]{0,1:T(8,128)S(1)}, f32[1024,256]{0,1:T(8,128)S(1)}, u32[]{:S(2)}, u32[]{:S(2)}) collective-permute-start(f32[1024,256]{0,1:T(8,128)S(1)} %get-tuple-element.23), channel_id=1, source_target_pairs={{0,4},{4,8},{8,12},{12,16},{16,20},{20,24},{24,28},{28,0},{1,5},{5... | collective-permute-start | bytes 3145736 | tf_op jit(solution)/shard_map/ppermute | solution.py:14
  152.6 57.4 %copy-start.5 = (f32[512,512]{0,1:T(8,128)}, f32[512,512]{0,1:T(8,128)S(1)}, u32[]{:S(2)}) copy-start(f32[512,512]{0,1:T(8,128)S(1)} %fusion.155) | copy-start | bytes 3145732
  167.5 169.2 %all-reduce.9.cloned.1.call-start = ((), (), s32[]{:S(2)}) async-start(), calls=%async_computation.2 | async-start | bytes 524288 | tf_op jit(solution)/shard_map/psum | solution.py:99
  168.3 47.8 %copy-start.42 = (f32[256,256]{0,1:T(8,128)}, f32[256,256]{0,1:T(8,128)S(1)}, u32[]{:S(2)}) copy-start(f32[256,256]{0,1:T(8,128)S(1)} %get-tuple-element.26) | copy-start | bytes 786436
  168.3 41.8 %collective-permute-start.1 = (f32[256,256]{0,1:T(8,128)S(1)}, f32[256,256]{0,1:T(8,128)S(1)}, u32[]{:S(2)}, u32[]{:S(2)}) collective-permute-start(f32[256,256]{0,1:T(8,128)S(1)} %get-tuple-element.27), channel_id=1, source_target_pairs={{0,4},{4,8},{8,12},{12,16},{16,20},{20,24},{24,28},{28,0},{1,5},{5... | collective-permute-start | bytes 786440 | tf_op jit(solution)/shard_map/ppermute | solution.py:14
  210.0 6.0 %copy-start.36 = (f32[256,256]{0,1:T(8,128)}, f32[256,256]{0,1:T(8,128)S(1)}, u32[]{:S(2)}) copy-start(f32[256,256]{0,1:T(8,128)S(1)} %copy.43) | copy-start | bytes 786436
  210.1 6.0 %copy-start.47 = (f32[256,256]{0,1:T(8,128)}, f32[256,256]{0,1:T(8,128)S(1)}, u32[]{:S(2)}) copy-start(f32[256,256]{0,1:T(8,128)S(1)} %collective-permute-done.1) | copy-start | bytes 786436
  210.1 6.0 %copy-start.35 = (f32[256,256]{0,1:T(8,128)S(1)}, f32[256,256]{0,1:T(8,128)}, u32[]{:S(2)}) copy-start(f32[256,256]{0,1:T(8,128)} %all-reduce.7.cloned.1.call-done) | copy-start | bytes 786436
  216.7 5.1 %copy-start.15 = (f32[512,512]{1,0:T(8,128)}, f32[512,512]{1,0:T(8,128)S(1)}, u32[]{:S(2)}) copy-start(f32[512,512]{1,0:T(8,128)S(1)} %copy.44) | copy-start | bytes 3145732
  261.2 3.6 copy-start.14
  276.5 16.1 %collective-permute-start.2 = (f32[1024,256]{0,1:T(8,128)S(1)}, f32[1024,256]{0,1:T(8,128)S(1)}, u32[]{:S(2)}, u32[]{:S(2)}) collective-permute-start(f32[1024,256]{0,1:T(8,128)S(1)} %get-tuple-element.21), channel_id=1, source_target_pairs={{0,4},{4,8},{8,12},{12,16},{16,20},{20,24},{24,28},{28,0},{1,5},{5... | collective-permute-start | bytes 3145736 | tf_op jit(solution)/shard_map/ppermute | solution.py:14
  280.4 17.1 %copy-start.6 = (f32[512,512]{0,1:T(8,128)S(1)}, f32[512,512]{0,1:T(8,128)}, u32[]{:S(2)}) copy-start(f32[512,512]{0,1:T(8,128)} %copy-done.5) | copy-start | bytes 3145732
  296.9 41.0 %collective-permute-start.3 = (f32[256,256]{0,1:T(8,128)}, f32[256,256]{0,1:T(8,128)S(1)}, u32[]{:S(2)}, u32[]{:S(2)}) collective-permute-start(f32[256,256]{0,1:T(8,128)} %get-tuple-element.30), channel_id=1, source_target_pairs={{0,4},{4,8},{8,12},{12,16},{16,20},{20,24},{24,28},{28,0},{1,5},{5... | collective-permute-start | bytes 786440 | tf_op jit(solution)/shard_map/ppermute | solution.py:14
  302.1 36.6 %copy-start.40 = (f32[256,256]{0,1:T(8,128)S(1)}, f32[256,256]{0,1:T(8,128)}, u32[]{:S(2)}) copy-start(f32[256,256]{0,1:T(8,128)} %get-tuple-element.29) | copy-start | bytes 786436
  337.8 6.9 %copy-start.38 = (f32[256,256]{0,1:T(8,128)}, f32[256,256]{0,1:T(8,128)S(1)}, u32[]{:S(2)}) copy-start(f32[256,256]{0,1:T(8,128)S(1)} %copy.54) | copy-start | bytes 786436
  338.6 6.2 %copy-start.34 = (f32[256,256]{0,1:T(8,128)S(1)}, f32[256,256]{0,1:T(8,128)}, u32[]{:S(2)}) copy-start(f32[256,256]{0,1:T(8,128)} %all-reduce.9.cloned.1.call-done) | copy-start | bytes 786436
  338.6 6.2 %copy-start.45 = (f32[256,256]{0,1:T(8,128)S(1)}, f32[256,256]{0,1:T(8,128)}, u32[]{:S(2)}) copy-start(f32[256,256]{0,1:T(8,128)} %copy-done.44) | copy-start | bytes 786436
  401.0 32.4 %collective-permute-start.4 = (f32[1024,256]{0,1:T(8,128)}, f32[1024,256]{0,1:T(8,128)}, u32[]{:S(2)}, u32[]{:S(2)}) collective-permute-start(f32[1024,256]{0,1:T(8,128)} %get-tuple-element.20), channel_id=1, source_target_pairs={{0,4},{4,8},{8,12},{12,16},{16,20},{20,24},{24,28},{28,0},{1,5},{5... | collective-permute-start | bytes 3145736 | tf_op jit(solution)/shard_map/ppermute | solution.py:14
  433.4 6.0 %copy-start.1 = (f32[1024,512]{1,0:T(8,128)S(1)}, f32[1024,512]{1,0:T(8,128)}, u32[]{:S(2)}) copy-start(f32[1024,512]{1,0:T(8,128)} %param.2) | copy-start | bytes 6291460
  (34 other events, 64.9 us)
Sparse Core Ops, SparseCore 0:
  13.4 55.1 all-reduce.4
  167.7 41.2 all-reduce.6
  295.5 41.2 all-reduce.8
where the time goes:
time: 452 us; the launch traced here: 446 us
  waiting for transfers between devices  144 us (32%)
  matrix products  142 us (31%)
  local copies, waits for them, and re-layouts  82.9 us (18%)
  other arithmetic  38.6 us (9%)
  between operations  21.1 us (5%)
  blocking collectives  17.8 us (4%)
    dot_general x54, matrix products, product(): jnp.dot(first, second, precision=highest, preferred_element_type=jnp.floa...  134 us
    psum x2, waiting for transfers between devices, on_device(): cross = lax.psum(local_product(keep, received), 'row')  69.6 us
    psum x1, waiting for transfers between devices, on_device(): gram = lax.psum(local_product(pair, pair), 'row')  49.7 us
    gather x6, local copies, waits for them, and re-layouts, sweep_rotation(): diag = jnp.diagonal(gram)  32.6 us
    ppermute x5, waiting for transfers between devices, from_behind(): return lax.ppermute(x, axis, [(i, (i + by) % count) for i in range(count)])  24.4 us
    psum x1, blocking collectives, tally_step(): return lax.psum((cross_sq, diag_sq), 'col')  17.8 us
    reduce_sum x6, other arithmetic, sweep_rotation(): scale = jnp.maximum(jnp.sqrt(jnp.sum(skew_raw * skew_raw)), 1.0)  13.9 us
    gather x3, local copies, waits for them, and re-layouts, rotate_local(): diag_sq = jnp.sum(jnp.diagonal(turned) ** 2)  13.6 us
  transfers between devices with their start and end apart: 8, of which 5 were waited for; matrix products, arithmetic and copies ran while one was open for 9% of the time, Pallas kernels for 0%

commit v1 on v0

--- a/solution.py
+++ b/solution.py
@@ -7,6 +7,12 @@
 STEPS = 3
 highest = lax.Precision.HIGHEST
 eps = 1e-06
+
+
+def summed_here(x, axis):
+    parts = lax.all_gather(x, axis, axis=0, tiled=False)
+    total = parts.sum(axis=0)
+    return total
 
 
 def from_behind(x, axis, by):
@@ -96,7 +102,7 @@
             keep_gram = jnp.where(flag, turned[:block, :block], turned[block:, block:])
             received, received_gram = from_behind((send, send_gram), "col", 1)
             pair = jnp.concatenate([keep, received], axis=1)
-            cross = lax.psum(local_product(keep, received), "row")
+            cross = summed_here(local_product(keep, received), "row")
             top_rows = jnp.concatenate([keep_gram, cross], axis=1)
             low_rows = jnp.concatenate([cross.T, received_gram], axis=1)
             gram = jnp.concatenate([top_rows, low_rows], axis=0)

time: 452 us -> 413 us (0.914)
  waiting for transfers between devices: 144 us -> 111 us
  local copies, waits for them, and re-layouts: 82.9 us -> 77.5 us
    psum x2 -> x0, waiting for transfers between devices: 69.6 us -> none  [on_device(): cross = lax.psum(local_product(keep, received), 'row')]
    all_gather x0 -> x2, waiting for transfers between devices: none -> 29.3 us  [summed_here(): parts = lax.all_gather(x, axis, axis=0, tiled=False)]
    ppermute x5, waiting for transfers between devices: 24.4 us -> 32 us  [from_behind(): return lax.ppermute(x, axis, [(i, (i + by) % count) for i in range(count)])]
    unnamed x101 -> x99, local copies, waits for them, and re-layouts: 9.29 us -> 8.52 us
  transfers between devices with their start and end apart: 8 -> 8, of which waited for: 5 -> 5; matrix products, arithmetic and copies ran while one was open for 9% -> 10% of each run, Pallas kernels for 0% -> 0%
where the time goes in v1:
time: 413 us; the launch traced here: 407 us
  matrix products  141 us (34%)
  waiting for transfers between devices  111 us (27%)
  local copies, waits for them, and re-layouts  77.5 us (19%)
  other arithmetic  38.1 us (9%)
  between operations  21.4 us (5%)
  blocking collectives  17.8 us (4%)
    dot_general x54, matrix products, product(): jnp.dot(first, second, precision=highest, preferred_element_type=jnp.floa...  133 us
    psum x1, waiting for transfers between devices, on_device(): gram = lax.psum(local_product(pair, pair), 'row')  49.6 us
    gather x6, local copies, waits for them, and re-layouts, sweep_rotation(): diag = jnp.diagonal(gram)  32.3 us
    ppermute x5, waiting for transfers between devices, from_behind(): return lax.ppermute(x, axis, [(i, (i + by) % count) for i in range(count)])  32 us
    all_gather x2, waiting for transfers between devices, summed_here(): parts = lax.all_gather(x, axis, axis=0, tiled=False)  29.3 us
    psum x1, blocking collectives, tally_step(): return lax.psum((cross_sq, diag_sq), 'col')  17.8 us
    reduce_sum x6, other arithmetic, sweep_rotation(): scale = jnp.maximum(jnp.sqrt(jnp.sum(skew_raw * skew_raw)), 1.0)  13.8 us
    gather x3, local copies, waits for them, and re-layouts, rotate_local(): diag_sq = jnp.sum(jnp.diagonal(turned) ** 2)  13.6 us
  transfers between devices with their start and end apart: 8, of which 5 were waited for; matrix products, arithmetic and copies ran while one was open for 10% of the time, Pallas kernels for 0%

profile of v1, /device:TPU:0, one launch (start us, length us, event | category | flops | bytes accessed | tf_op | source)
XLA Modules:
  0.0 407.2 jit_solution(9720631350875730459)
XLA Ops:
  8.8 4.5 %fusion.148 = f32[512,512]{1,0:T(8,128)} fusion(f32[1024,512]{1,0:T(8,128)S(1)} %copy-done), kind=kOutput, calls=%fused_computation.235 | convolution fusion | flops 3221225472 | bytes 3145728 | tf_op jit(solution)/shard_map/dot_general | solution.py:53
  19.0 49.6 %all-reduce.3.cloned.1.call-done = f32[512,512]{1,0:T(8,128)} async-done(((f32[512,512]{1,0:T(8,128)}), f32[512,512]{1,0:T(8,128)}) %all-reduce.3.cloned.1.call-update) | async-done | bytes 1048592 | tf_op jit(solution)/shard_map/psum | solution.py:91
  68.7 9.1 %gather_fusion = f32[512]{0:T(512)S(1)} fusion(f32[512,512]{1,0:T(8,128)} %all-reduce.3.cloned.1.call-done, s32[512]{0:T(512)S(1)} %bitcast.139), kind=kCustom, calls=%fused_computation | custom fusion | bytes 8192 | tf_op jit(solution)/shard_map/jit(diagonal)/cond/branch_0_fun/gather | solution.py:33
  90.0 4.2 %fusion.141 = f32[512,512]{1,0:T(8,128)S(1)} fusion(f32[]{:T(128)S(6)} %max.18, f32[512,512]{1,0:T(8,128)} %divide_multiply_fusion, f32[512,512]{0,1:T(8,128)} %copy.59), kind=kOutput, calls=%fused_computation.230 | convolution fusion | flops 1611137024 | bytes 3145732 | tf_op jit(solution)/shard_map/dot_general | solution.py:24
  107.9 4.5 %gather_fusion.1 = f32[512]{0:T(512)S(1)} fusion(f32[512,512]{1,0:T(8,128)S(1)} %fusion.151, s32[512]{0:T(512)S(1)} %bitcast.140), kind=kCustom, calls=%fused_computation.1 | custom fusion | bytes 8192 | tf_op jit(solution)/shard_map/jit(diagonal)/cond/branch_0_fun/gather | solution.py:33
  118.1 5.2 %fusion.87 = f32[512,512]{1,0:T(8,128)S(1)} fusion(f32[512,512]{0,1:T(8,128)} %get-tuple-element.20, f32[]{:T(128)S(6)} %max.19), kind=kOutput, calls=%fused_computation.160 | convolution fusion | flops 1610874880 | bytes 2097156 | tf_op jit(solution)/shard_map/dot_general | solution.py:24
  129.7 3.6 fusion.35
  142.5 6.7 %convolution_bitcast_fusion = f32[1024,512]{0,1:T(8,128)S(1)} fusion(f32[512,512]{1,0:T(8,128)S(1)} %fusion.153, f32[1024,512]{1,0:T(8,128)S(1)} %copy-done), kind=kOutput, calls=%fused_computation.50 | convolution fusion | flops 3221225472 | bytes 5242880 | tf_op jit(solution)/shard_map/dot_general | solution.py:24
  149.5 16.0 %collective-permute-done = f32[1024,256]{0,1:T(8,128)S(1)} collective-permute-done((f32[1024,256]{0,1:T(8,128)S(1)}, f32[1024,256]{0,1:T(8,128)S(1)}, u32[]{:S(2)}, u32[]{:S(2)}) %collective-permute-start) | collective-permute-done | bytes 1048608 | tf_op jit(solution)/shard_map/ppermute | solution.py:20
  173.6 19.5 %all-gather.5.cloned.1.call-done = f32[1024,256]{1,0:T(8,128)} async-done(((f32[256,256]{1,0:T(8,128)}), f32[1024,256]{1,0:T(8,128)}) %all-gather.5.cloned.1.call-update) | async-done | bytes 1048592 | tf_op jit(solution)/shard_map/all_gather | solution.py:13
  194.7 4.7 %gather_fusion.2 = f32[512]{0:T(512)S(1)} fusion(f32[512,512]{0,1:T(8,128)S(1)} %maximum_maximum_fusion, s32[512]{0:T(512)S(1)} %bitcast.141), kind=kCustom, calls=%fused_computation.2 | custom fusion | bytes 8192 | tf_op jit(solution)/shard_map/jit(diagonal)/cond/branch_0_fun/gather | solution.py:33
  223.1 4.5 %gather_fusion.3 = f32[512]{0:T(512)S(1)} fusion(f32[512,512]{1,0:T(8,128)S(1)} %fusion.158, s32[512]{0:T(512)S(1)} %bitcast.142), kind=kCustom, calls=%fused_computation.3 | custom fusion | bytes 8192 | tf_op jit(solution)/shard_map/jit(diagonal)/cond/branch_0_fun/gather | solution.py:33
  233.0 5.1 %fusion.88 = f32[512,512]{1,0:T(8,128)S(1)} fusion(f32[512,512]{0,1:T(8,128)} %get-tuple-element.18, f32[]{:T(128)S(6)} %max.21), kind=kOutput, calls=%fused_computation.161 | convolution fusion | flops 1610874880 | bytes 2097156 | tf_op jit(solution)/shard_map/dot_general | solution.py:24
  242.4 3.6 fusion.25
  257.8 16.0 %collective-permute-done.2 = f32[1024,256]{0,1:T(8,128)S(1)} collective-permute-done((f32[1024,256]{0,1:T(8,128)S(1)}, f32[1024,256]{0,1:T(8,128)S(1)}, u32[]{:S(2)}, u32[]{:S(2)}) %collective-permute-start.2) | collective-permute-done | bytes 1048608 | tf_op jit(solution)/shard_map/ppermute | solution.py:20
  281.8 4.5 %gather_fusion.6 = f32[512]{0:T(512)S(1)} fusion(f32[512,512]{0,1:T(8,128)S(1)} %copy-done.9, s32[512]{0:T(512)S(1)} %bitcast.143), kind=kCustom, calls=%fused_computation.6 | custom fusion | bytes 8192 | tf_op jit(solution)/shard_map/jit(diagonal)/cond/branch_0_fun/gather | solution.py:70
  287.0 4.5 %gather_fusion.7 = f32[512]{0:T(512)S(1)} fusion(f32[512,512]{0,1:T(8,128)S(1)} %fusion.162, s32[512]{0:T(512)S(1)} %bitcast.144), kind=kCustom, calls=%fused_computation.7 | custom fusion | bytes 8192 | tf_op jit(solution)/shard_map/jit(diagonal)/cond/branch_0_fun/gather | solution.py:70
  291.6 9.9 %all-gather.7.cloned.1.call-done = f32[1024,256]{1,0:T(8,128)} async-done(((f32[256,256]{1,0:T(8,128)}), f32[1024,256]{1,0:T(8,128)}) %all-gather.7.cloned.1.call-update) | async-done | bytes 1048592 | tf_op jit(solution)/shard_map/all_gather | solution.py:13
  303.1 5.0 %gather_fusion.4 = f32[512]{0:T(512)S(1)} fusion(f32[512,512]{0,1:T(8,128)S(1)} %maximum_maximum_fusion.1, s32[512]{0:T(512)S(1)} %bitcast.145), kind=kCustom, calls=%fused_computation.4 | custom fusion | bytes 8192 | tf_op jit(solution)/shard_map/jit(diagonal)/cond/branch_0_fun/gather | solution.py:33
  326.1 4.5 %gather_fusion.5 = f32[512]{0:T(512)S(1)} fusion(f32[512,512]{1,0:T(8,128)S(1)} %fusion.165, s32[512]{0:T(512)S(1)} %bitcast.146), kind=kCustom, calls=%fused_computation.5 | custom fusion | bytes 8192 | tf_op jit(solution)/shard_map/jit(diagonal)/cond/branch_0_fun/gather | solution.py:33
  341.7 3.7 fusion.89
  366.5 4.5 %gather_fusion.8 = f32[512]{0:T(512)S(1)} fusion(f32[512,512]{1,0:T(8,128)S(1)} %fusion.169, s32[512]{0:T(512)S(1)} %bitcast.147), kind=kCustom, calls=%fused_computation.8 | custom fusion | bytes 8192 | tf_op jit(solution)/shard_map/jit(diagonal)/cond/branch_0_fun/gather | solution.py:70
  372.4 17.8 %all-reduce = (f32[1]{0:T(128)}, f32[1]{0:T(128)}, f32[1]{0:T(128)}, f32[1]{0:T(128)}, f32[1]{0:T(128)}, /*index=5*/f32[1]{0:T(128)}) all-reduce(f32[1]{0:T(128)} %bitcast.20, f32[1]{0:T(128)} %bitcast.19, f32[1]{0:T(128)} %bitcast.18, f32[1]{0:T(128)} %bitcast.17, f32[1]{0:T(128)} %bitcast.16, ...), channel_id=1, replica_groups=mesh['col'=8,'row'=4] {'col'}, use_global_device_ids=true, to_apply=%region_23.24 | all-reduce | flops 6 | bytes 48 | tf_op jit(solution)/shard_map/psum | solution.py:75
  390.2 4.2 %fusion.96 = f32[3]{0:T(128)} fusion(f32[1]{0:T(128)} %get-tuple-element.11, f32[1]{0:T(128)} %get-tuple-element.12, f32[1]{0:T(128)} %get-tuple-element.13, f32[1]{0:T(128)} %get-tuple-element.14, f32[1]{0:T(128)} %get-tuple-element.15, f32[1]{0:T(128)} %get-tuple-element.16), kind=kLoop, calls=%fused_computation.185 | loop fusion | flops 15 | bytes 36 | tf_op jit(solution)/shard_map/log | solution.py:81
  (209 shorter events, 170.3 us)
Async XLA Ops:
  7.2 61.5 %all-reduce.3.cloned.1.call-start = ((), (), s32[]{:S(2)}) async-start(), calls=%async_computation | async-start | bytes 2097152 | tf_op jit(solution)/shard_map/psum | solution.py:91
  13.3 179.8 %all-gather.5.cloned.1.call-start = ((), (), s32[]{:S(2)}) async-start(), calls=%async_computation.1 | async-start | bytes 1310720 | tf_op jit(solution)/shard_map/all_gather | solution.py:13
  77.7 3.7 copy-start.4
  129.7 3.6 copy-start.18
  149.4 18.9 %copy-start.15 = (f32[1024,256]{0,1:T(8,128)}, f32[1024,256]{0,1:T(8,128)S(1)}, u32[]{:S(2)}) copy-start(f32[1024,256]{0,1:T(8,128)S(1)} %get-tuple-element.26) | copy-start | bytes 3145732
  149.4 18.9 %copy-start.3 = (f32[512,512]{1,0:T(8,128)S(1)}, f32[512,512]{1,0:T(8,128)}, u32[]{:S(2)}) copy-start(f32[512,512]{1,0:T(8,128)} %copy-done.2) | copy-start | bytes 3145732
  149.4 16.1 %collective-permute-start = (f32[1024,256]{0,1:T(8,128)S(1)}, f32[1024,256]{0,1:T(8,128)S(1)}, u32[]{:S(2)}, u32[]{:S(2)}) collective-permute-start(f32[1024,256]{0,1:T(8,128)S(1)} %get-tuple-element.25), channel_id=1, source_target_pairs={{0,4},{4,8},{8,12},{12,16},{16,20},{20,24},{24,28},{28,0},{1,5},{5... | collective-permute-start | bytes 3145736 | tf_op jit(solution)/shard_map/ppermute | solution.py:20
  168.3 133.2 %all-gather.7.cloned.1.call-start = ((), (), s32[]{:S(2)}) async-start(), calls=%async_computation.2 | async-start | bytes 1310720 | tf_op jit(solution)/shard_map/all_gather | solution.py:13
  172.1 22.6 %copy-start.8 = (f32[512,512]{0,1:T(8,128)}, f32[512,512]{0,1:T(8,128)S(1)}, u32[]{:S(2)}) copy-start(f32[512,512]{0,1:T(8,128)S(1)} %fusion.155) | copy-start | bytes 3145732
  173.0 26.5 %copy-start.42 = (f32[256,256]{0,1:T(8,128)}, f32[256,256]{0,1:T(8,128)S(1)}, u32[]{:S(2)}) copy-start(f32[256,256]{0,1:T(8,128)S(1)} %get-tuple-element.28) | copy-start | bytes 786436
  173.0 21.6 %collective-permute-start.1 = (f32[256,256]{0,1:T(8,128)S(1)}, f32[256,256]{0,1:T(8,128)S(1)}, u32[]{:S(2)}, u32[]{:S(2)}) collective-permute-start(f32[256,256]{0,1:T(8,128)S(1)} %get-tuple-element.29), channel_id=1, source_target_pairs={{0,4},{4,8},{8,12},{12,16},{16,20},{20,24},{24,28},{28,0},{1,5},{5... | collective-permute-start | bytes 786440 | tf_op jit(solution)/shard_map/ppermute | solution.py:20
  194.6 4.9 %copy-start.36 = (f32[256,256]{0,1:T(8,128)}, f32[256,256]{0,1:T(8,128)S(1)}, u32[]{:S(2)}) copy-start(f32[256,256]{0,1:T(8,128)S(1)} %copy.66) | copy-start | bytes 786436
  194.6 4.9 %copy-start.46 = (f32[256,256]{0,1:T(8,128)}, f32[256,256]{0,1:T(8,128)S(1)}, u32[]{:S(2)}) copy-start(f32[256,256]{0,1:T(8,128)S(1)} %collective-permute-done.1) | copy-start | bytes 786436
  200.1 5.2 %copy-start.21 = (f32[512,512]{1,0:T(8,128)}, f32[512,512]{1,0:T(8,128)S(1)}, u32[]{:S(2)}) copy-start(f32[512,512]{1,0:T(8,128)S(1)} %copy.67) | copy-start | bytes 3145732
  223.1 5.9 %copy-start.12 = (f32[512,512]{0,1:T(8,128)S(1)}, f32[512,512]{0,1:T(8,128)}, u32[]{:S(2)}) copy-start(f32[512,512]{0,1:T(8,128)} %copy.62) | copy-start | bytes 3145732
  242.4 3.6 copy-start.20
  257.8 16.1 %copy-start.13 = (f32[1024,256]{0,1:T(8,128)}, f32[1024,256]{0,1:T(8,128)S(1)}, u32[]{:S(2)}) copy-start(f32[1024,256]{0,1:T(8,128)S(1)} %get-tuple-element.24) | copy-start | bytes 3145732
  257.8 16.1 %collective-permute-start.2 = (f32[1024,256]{0,1:T(8,128)S(1)}, f32[1024,256]{0,1:T(8,128)S(1)}, u32[]{:S(2)}, u32[]{:S(2)}) collective-permute-start(f32[1024,256]{0,1:T(8,128)S(1)} %get-tuple-element.23), channel_id=1, source_target_pairs={{0,4},{4,8},{8,12},{12,16},{16,20},{20,24},{24,28},{28,0},{1,5},{5... | collective-permute-start | bytes 3145736 | tf_op jit(solution)/shard_map/ppermute | solution.py:20
  281.2 26.9 %copy-start.40 = (f32[256,256]{0,1:T(8,128)}, f32[256,256]{0,1:T(8,128)S(1)}, u32[]{:S(2)}) copy-start(f32[256,256]{0,1:T(8,128)S(1)} %get-tuple-element.31) | copy-start | bytes 786436
  281.2 21.8 %collective-permute-start.3 = (f32[256,256]{0,1:T(8,128)S(1)}, f32[256,256]{0,1:T(8,128)S(1)}, u32[]{:S(2)}, u32[]{:S(2)}) collective-permute-start(f32[256,256]{0,1:T(8,128)S(1)} %get-tuple-element.32), channel_id=1, source_target_pairs={{0,4},{4,8},{8,12},{12,16},{16,20},{20,24},{24,28},{28,0},{1,5},{5... | collective-permute-start | bytes 786440 | tf_op jit(solution)/shard_map/ppermute | solution.py:20
  302.9 5.2 %copy-start.38 = (f32[256,256]{0,1:T(8,128)}, f32[256,256]{0,1:T(8,128)S(1)}, u32[]{:S(2)}) copy-start(f32[256,256]{0,1:T(8,128)S(1)} %copy.76) | copy-start | bytes 786436
  302.9 5.1 %copy-start.44 = (f32[256,256]{0,1:T(8,128)}, f32[256,256]{0,1:T(8,128)S(1)}, u32[]{:S(2)}) copy-start(f32[256,256]{0,1:T(8,128)S(1)} %collective-permute-done.3) | copy-start | bytes 786436
  362.1 32.4 %collective-permute-start.4 = (f32[1024,256]{0,1:T(8,128)}, f32[1024,256]{0,1:T(8,128)}, u32[]{:S(2)}, u32[]{:S(2)}) collective-permute-start(f32[1024,256]{0,1:T(8,128)} %get-tuple-element.22), channel_id=1, source_target_pairs={{0,4},{4,8},{8,12},{12,16},{16,20},{20,24},{24,28},{28,0},{1,5},{5... | collective-permute-start | bytes 3145736 | tf_op jit(solution)/shard_map/ppermute | solution.py:20
  394.5 6.0 %copy-start.1 = (f32[1024,512]{1,0:T(8,128)S(1)}, f32[1024,512]{1,0:T(8,128)}, u32[]{:S(2)}) copy-start(f32[1024,512]{1,0:T(8,128)} %param.2) | copy-start | bytes 6291460
  (33 other events, 66.2 us)
Sparse Core Ops, SparseCore 0:
  13.4 55.1 all-reduce.2
  168.4 24.6 all-gather.4
  276.7 24.6 all-gather.6
